TPU v7x, 32 devices: a whole 2x2x4 slice. The times are simulated.
32 devices in a mesh: groups: 2 (over x), wide: 16 (over z, y, core).
Axes of the slice: x: 2, y: 2, z: 4, core: 2. Of those that a mesh axis runs over, the one named last changes fastest.
Arguments:
- prefix_hidden: bfloat16 [32, 256, 8192], P(('groups', 'wide')), parts along dimension 0, may hold values from -6 to 6
- prefix_lengths: int32 [32], P(('groups', 'wide')), parts along dimension 0, may hold values from 64 to 256
- action_noise: float32 [32, 50, 32], P(('groups', 'wide')), parts along dimension 0, may hold values from -4 to 4
- prefix_gain: float32 [8192], replicated, may hold values from 0.1 to 1.9
- key_weight: bfloat16 [8192, 512], P('wide'), may hold values from -0.0625 to 0.0625
- value_weight: bfloat16 [8192, 512], P('wide'), may hold values from -0.0625 to 0.0625
- input_weight: float32 [32, 1024], replicated, may hold values from -1 to 1
- expert_gain: float32 [1024], replicated, may hold values from 0.1 to 1.9
- expert_query: bfloat16 [1024, 1024], P('wide'), may hold values from -0.1875 to 0.1875
- expert_key: bfloat16 [1024, 512], P('wide'), may hold values from -5.3125 to 5.3125
- expert_value: bfloat16 [1024, 512], P('wide'), may hold values from -0.1875 to 0.1875
- expert_output: bfloat16 [1024, 1024], P('wide'), may hold values from -0.1875 to 0.1875
- final_gain: float32 [1024], replicated, may hold values from 0.1 to 1.9
- output_weight: bfloat16 [1024, 32], replicated, may hold values from -0.1875 to 0.1875
Outputs:
- actions: float32 [32, 50, 32], P(('groups', 'wide')), parts along dimension 0
There are 2 independent parts, one for each index of `groups`. A program takes and returns all parts, laid end to end along the dimension named above; an argument that names none is the same for every part. Nothing has to cross between parts.
Inputs may be any that keep to these rules, and one draw needn't show every extreme that they name: `prefix_lengths`: positions at or after a sample's length are padding and take no part.
All inputs are finite; a program needn't handle non-finite values.
Results may differ from a plain program's by a relative error of at most 0.0075.
Values may be sent and summed in bfloat16 or wider, within the bound.
A program may use at most 128 MiB of HBM per device.

v0:
```python
import jax
import jax.numpy as jnp
from jax import lax
from jax.sharding import PartitionSpec as P

HEAD = 128
STEPS = 4
rope_base = 1000000.0
norm_eps = 1e-06


def normalize(values, norm_gain):
    mean_square = jnp.mean(values * values, axis=-1, keepdims=True)
    return values * lax.rsqrt(mean_square + norm_eps) * norm_gain


def rotate(values, positions):
    half_width = values.shape[-1] // 2
    inv_freqs = rope_base ** (-jnp.arange(half_width, dtype=jnp.float32) * 2.0 / values.shape[-1])
    angles = positions[:, None] * inv_freqs[None, :]
    cosine = jnp.cos(angles)[:, None, :]
    sine_part = jnp.sin(angles)[:, None, :]
    first_half = values[..., :half_width]
    second = values[..., half_width:]
    return jnp.concatenate(
        [first_half * cosine - second * sine_part, second * cosine + first_half * sine_part], -1
    )


def time_embedding(time_value, embed_width):
    half_width = embed_width // 2
    fraction = jnp.arange(half_width, dtype=jnp.float32) / (half_width - 1)
    period = 0.004 * (4.0 / 0.004) ** fraction
    angles = time_value * (2.0 * jnp.pi) / period
    return jnp.concatenate([jnp.sin(angles), jnp.cos(angles)])


def attend(queries, key_cache, value_cache, action_keys, action_values, is_valid):
    span_rows = queries.shape[0]
    groups = key_cache.shape[1] // HEAD
    group_ratio = queries.shape[1] // key_cache.shape[1]
    query_heads = queries.reshape(span_rows, groups, group_ratio, HEAD)
    prefix_keys = key_cache.reshape(-1, groups, HEAD)
    prefix_values = value_cache.reshape(-1, groups, HEAD)
    own_keys = action_keys.reshape(span_rows, groups, HEAD)
    own_values = action_values.reshape(span_rows, groups, HEAD)
    prefix_scores = jnp.einsum(
        "cgrh,pgh->grcp", query_heads, prefix_keys, preferred_element_type=jnp.float32
    )
    prefix_scores = jnp.where(is_valid[None, None, None, :], prefix_scores, -1e30)
    own_scores = jnp.einsum(
        "cgrh,ngh->grcn", query_heads, own_keys, preferred_element_type=jnp.float32
    )
    row_max = jnp.maximum(jnp.max(prefix_scores, -1), jnp.max(own_scores, -1))[..., None]
    prefix_exp = jnp.exp(prefix_scores - row_max)
    own_exp = jnp.exp(own_scores - row_max)
    prob_total = jnp.sum(prefix_exp, -1, keepdims=True) + jnp.sum(own_exp, -1, keepdims=True)
    prefix_prob = (prefix_exp / prob_total).astype(jnp.bfloat16)
    own_prob = (own_exp / prob_total).astype(jnp.bfloat16)
    attn_mixed = jnp.einsum(
        "grcp,pgh->cgrh", prefix_prob, prefix_values, preferred_element_type=jnp.float32
    )
    attn_mixed = attn_mixed + jnp.einsum(
        "grcn,ngh->cgrh", own_prob, own_values, preferred_element_type=jnp.float32
    )
    return attn_mixed.reshape(span_rows, -1).astype(jnp.bfloat16)


def expert_steps(
    noise_rows,
    length,
    input_weight,
    expert_gain,
    query_w,
    key_w,
    value_w,
    output_w,
    final_gain,
    output_weight,
    key_cache,
    value_cache,
):
    span_rows = noise_rows.shape[0]
    is_valid = jnp.arange(key_cache.shape[0], dtype=jnp.int32) < length
    positions = length.astype(jnp.float32) + jnp.arange(span_rows, dtype=jnp.float32)
    action_state = noise_rows
    for step_idx in range(STEPS):
        time_value = 1.0 - step_idx / STEPS
        hidden = jnp.dot(
            action_state,
            input_weight,
            precision=lax.Precision.HIGHEST,
            preferred_element_type=jnp.float32,
        )
        hidden = hidden + time_embedding(time_value, input_weight.shape[1])[None, :]
        normed = normalize(hidden, expert_gain).astype(jnp.bfloat16)
        raw_queries = jnp.dot(normed, query_w, preferred_element_type=jnp.float32)
        queries = rotate(raw_queries.reshape(span_rows, -1, HEAD), positions).reshape(span_rows, -1)
        queries = (queries * HEAD ** (-0.5)).astype(jnp.bfloat16)
        raw_keys = jnp.dot(normed, key_w, preferred_element_type=jnp.float32)
        action_keys = (
            rotate(raw_keys.reshape(span_rows, -1, HEAD), positions)
            .reshape(span_rows, -1)
            .astype(jnp.bfloat16)
        )
        action_values = jnp.dot(normed, value_w, preferred_element_type=jnp.float32).astype(
            jnp.bfloat16
        )
        attn_mixed = attend(queries, key_cache, value_cache, action_keys, action_values, is_valid)
        hidden = hidden + jnp.dot(attn_mixed, output_w, preferred_element_type=jnp.float32)
        final_normed = normalize(hidden, final_gain).astype(jnp.bfloat16)
        velocity = jnp.dot(final_normed, output_weight, preferred_element_type=jnp.float32)
        action_state = action_state - velocity / STEPS
    return action_state


def shards(
    prefix_hidden,
    prefix_lengths,
    action_noise,
    prefix_gain,
    key_weight,
    value_weight,
    input_weight,
    expert_gain,
    expert_query,
    expert_key,
    expert_value,
    expert_output,
    final_gain,
    output_weight,
):
    gathered = (
        lax.all_gather(expert_query, "wide", axis=0, tiled=True),
        lax.all_gather(expert_key, "wide", axis=0, tiled=True),
        lax.all_gather(expert_value, "wide", axis=0, tiled=True),
        lax.all_gather(expert_output, "wide", axis=0, tiled=True),
    )
    hidden = prefix_hidden[0]
    row_count = hidden.shape[0]
    normed = normalize(hidden.astype(jnp.float32), prefix_gain).astype(jnp.bfloat16)
    stacked = jnp.stack([key_weight, value_weight], 0)
    projected = jnp.einsum(
        "pd,kdc->pkc",
        normed,
        lax.all_gather(stacked, "wide", axis=1, tiled=True),
        preferred_element_type=jnp.float32,
    )
    positions = jnp.arange(row_count, dtype=jnp.float32)
    key_cache = (
        rotate(projected[:, 0].reshape(row_count, -1, HEAD), positions)
        .reshape(row_count, -1)
        .astype(jnp.bfloat16)
    )
    value_cache = projected[:, 1].astype(jnp.bfloat16)
    query_w, key_w, value_w, output_w = gathered
    action_state = expert_steps(
        action_noise[0],
        prefix_lengths[0],
        input_weight,
        expert_gain,
        query_w,
        key_w,
        value_w,
        output_w,
        final_gain,
        output_weight,
        key_cache,
        value_cache,
    )
    return action_state[None]


def solution(mesh):
    placed = (
        P(("groups", "wide"), None, None),
        P(("groups", "wide")),
        P(("groups", "wide"), None, None),
        P(),
        P("wide", None),
        P("wide", None),
        P(),
        P(),
        P("wide", None),
        P("wide", None),
        P("wide", None),
        P("wide", None),
        P(),
        P(),
    )
    return jax.shard_map(
        shards,
        mesh=mesh,
        in_specs=placed,
        out_specs=P(("groups", "wide"), None, None),
        check_vma=False,
    )
```

profile of v0, /device:TPU:0, one launch (start us, length us, event | category | flops | bytes accessed | tf_op | source)
XLA Modules:
  0.0 368.0 jit_solution(7898720133912089493)
XLA Ops:
  8.8 2.3 pad_maximum_fusion
  12.0 3.1 fusion
  19.0 31.2 %all-gather.10.cloned.1.call-done = bf16[1024,512]{1,0:T(8,128)(2,1)} async-done(((bf16[64,512]{1,0:T(8,128)(2,1)}), bf16[1024,512]{1,0:T(8,128)(2,1)}) %all-gather.10.cloned.1.call-update) | async-done | bytes 1048592 | tf_op jit(solution)/shard_map/all_gather | solution.py:135
  50.2 1.5 fusion.107
  51.9 37.4 %all-gather.12.cloned.1.call-done = bf16[1024,512]{1,0:T(8,128)(2,1)} async-done(((bf16[64,512]{1,0:T(8,128)(2,1)}), bf16[1024,512]{1,0:T(8,128)(2,1)}) %all-gather.12.cloned.1.call-update) | async-done | bytes 1048592 | tf_op jit(solution)/shard_map/all_gather | solution.py:136
  89.2 1.5 convolution_convert_fusion.3
  91.4 40.4 %all-gather.8.cloned.1.call-done = bf16[1024,1024]{1,0:T(8,128)(2,1)} async-done(((bf16[64,1024]{1,0:T(8,128)(2,1)}), bf16[1024,1024]{1,0:T(8,128)(2,1)}) %all-gather.8.cloned.1.call-update) | async-done | bytes 2097168 | tf_op jit(solution)/shard_map/all_gather | solution.py:134
  131.9 2.1 fusion.106
  134.6 124.5 %all-gather.6.cloned.1.call-done = bf16[2,8192,512]{2,1,0:T(8,128)(2,1)} async-done(((bf16[2,512,512]{2,1,0:T(8,128)(2,1)}), bf16[2,8192,512]{2,1,0:T(8,128)(2,1)}) %all-gather.6.cloned.1.call-update) | async-done | bytes 16777232 | tf_op jit(solution)/shard_map/all_gather | solution.py:146
  259.1 9.5 %fusion.4 = f32[256,2,512]{2,0,1:T(8,128)S(1)} fusion(bf16[2,8192,512]{2,1,0:T(8,128)(2,1)} %all-gather.6.cloned.1.call-done, bf16[1,256,8192]{2,1,0:T(8,128)(2,1)} %param.14, f32[8192]{0:T(1024)S(1)} %copy-done.58, f32[256]{0:T(256)S(1)} %add_rsqrt_fusion), kind=kOutput, calls=%fused_computation.6 | convolution fusion | flops 4303355904 | bytes 22053888 | tf_op jit(solution)/shard_map/pd,kdc->pkc/dot_general | solution.py:143
  271.2 29.5 %all-gather.14.cloned.1.call-done = bf16[1024,1024]{1,0:T(8,128)(2,1)} async-done(((bf16[64,1024]{1,0:T(8,128)(2,1)}), bf16[1024,1024]{1,0:T(8,128)(2,1)}) %all-gather.14.cloned.1.call-update) | async-done | bytes 2097168 | tf_op jit(solution)/shard_map/all_gather | solution.py:137
  300.8 2.2 multiply_reduce_fusion.6
  306.0 1.7 fusion.100
  307.7 0.9 fusion.109
  308.6 1.6 reshape.311
  310.2 1.1 fusion.96
  311.3 0.8 subtract_convert_fusion.3
  312.1 1.2 fusion.101
  314.1 1.3 fusion.27
  315.5 2.1 fusion.31
  317.6 0.9 convolution_convert_fusion.2
  318.5 1.5 reshape.312
  320.0 1.3 fusion.19
  321.3 0.7 copy.50
  322.0 1.6 convert_element_type.174
  323.6 2.2 multiply_reduce_fusion.4
  329.0 1.1 fusion.102
  330.1 0.9 fusion.111
  331.1 1.6 reshape.314
  332.6 1.1 fusion.95
  333.7 0.8 subtract_convert_fusion.2
  334.5 1.2 fusion.103
  335.7 1.4 fusion.28
  337.2 2.1 fusion.32
  339.3 0.9 convolution_convert_fusion.1
  340.2 1.5 reshape.315
  341.7 1.3 fusion.18
  343.0 0.7 copy.57
  343.7 1.6 convert_element_type.184
  345.3 2.2 multiply_reduce_fusion.2
  347.6 1.0 fusion.23
  348.6 1.2 multiply_reduce_fusion.1
  350.5 0.8 multiply_convert_fusion.1
  354.5 2.3 fusion.33
  356.7 0.9 convolution_convert_fusion
  357.7 0.9 reshape.318
  358.5 1.3 fusion.17
  360.6 0.8 fusion.22
  (221 shorter events, 21.2 us)
Async XLA Ops:
  6.5 9.1 %copy-start = (f32[32,1024]{1,0:T(8,128)S(1)}, f32[32,1024]{1,0:T(8,128)}, u32[]{:S(2)}) copy-start(f32[32,1024]{1,0:T(8,128)} %param.20) | copy-start | bytes 393220
  6.5 43.7 %all-gather.10.cloned.1.call-start = ((), (), s32[]{:S(2)}) async-start(), calls=%async_computation.2 | async-start | bytes 1114112 | tf_op jit(solution)/shard_map/all_gather | solution.py:135
  7.3 82.0 %all-gather.12.cloned.1.call-start = ((), (), s32[]{:S(2)}) async-start(), calls=%async_computation.3 | async-start | bytes 1114112 | tf_op jit(solution)/shard_map/all_gather | solution.py:136
  8.0 123.8 %all-gather.8.cloned.1.call-start = ((), (), s32[]{:S(2)}) async-start(), calls=%async_computation.1 | async-start | bytes 2228224 | tf_op jit(solution)/shard_map/all_gather | solution.py:134
  8.7 250.4 %all-gather.6.cloned.1.call-start = ((), (), s32[]{:S(2)}) async-start(), calls=%async_computation | async-start | bytes 17825792 | tf_op jit(solution)/shard_map/all_gather | solution.py:146
  11.1 289.7 %all-gather.14.cloned.1.call-start = ((), (), s32[]{:S(2)}) async-start(), calls=%async_computation.4 | async-start | bytes 2228224 | tf_op jit(solution)/shard_map/all_gather | solution.py:137
  11.9 3.7 %copy-start.44 = (f32[1,50,32]{1,2,0:T(8,128)S(1)}, f32[1,50,32]{1,2,0:T(8,128)}, u32[]{:S(2)}) copy-start(f32[1,50,32]{1,2,0:T(8,128)} %param.16) | copy-start | bytes 19204
  12.0 6.9 %copy-start.41 = (f32[1024]{0:T(1024)S(1)}, f32[1024]{0:T(1024)}, u32[]{:S(2)}) copy-start(f32[1024]{0:T(1024)} %param.21) | copy-start | bytes 12292
  16.1 117.8 %copy-start.17 = (f32[50,1024]{1,0:T(8,128)}, f32[50,1024]{1,0:T(8,128)S(1)}, u32[]{:S(2)}) copy-start(f32[50,1024]{1,0:T(8,128)S(1)} %get-tuple-element.38) | copy-start | bytes 614404
  17.0 117.0 %copy-start.7 = (f32[50,64]{1,0:T(8,128)}, f32[50,64]{1,0:T(8,128)S(1)}, u32[]{:S(2)}) copy-start(f32[50,64]{1,0:T(8,128)S(1)} %get-tuple-element.33) | copy-start | bytes 38404
  17.0 117.0 %copy-start.12 = (f32[50,64]{1,0:T(8,128)}, f32[50,64]{1,0:T(8,128)S(1)}, u32[]{:S(2)}) copy-start(f32[50,64]{1,0:T(8,128)S(1)} %get-tuple-element.34) | copy-start | bytes 38404
  17.0 252.6 %copy-start.53 = (pred[256]{0:T(512)(128)(4,1)}, pred[256]{0:T(512)(128)(4,1)S(1)}, u32[]{:S(2)}) copy-start(pred[256]{0:T(512)(128)(4,1)S(1)} %iota_compare_fusion) | copy-start | bytes 772
  91.4 167.7 %copy-start.58 = (f32[8192]{0:T(1024)S(1)}, f32[8192]{0:T(1024)}, u32[]{:S(2)}) copy-start(f32[8192]{0:T(1024)} %param.17) | copy-start | bytes 98308
  270.1 30.6 %copy-start.18 = (f32[50,1024]{1,0:T(8,128)S(1)}, f32[50,1024]{1,0:T(8,128)}, u32[]{:S(2)}) copy-start(f32[50,1024]{1,0:T(8,128)} %copy-done.17) | copy-start | bytes 614404
  270.8 32.2 %copy-start.30 = (bf16[1024,32]{0,1:T(8,128)(2,1)S(1)}, bf16[1024,32]{0,1:T(8,128)(2,1)}, u32[]{:S(2)}) copy-start(bf16[1024,32]{0,1:T(8,128)(2,1)} %param.27) | copy-start | bytes 196612
  270.8 32.2 %copy-start.45 = (f32[1,50,32]{1,2,0:T(8,128)S(1)}, f32[1,50,32]{1,2,0:T(8,128)}, u32[]{:S(2)}) copy-start(f32[1,50,32]{1,2,0:T(8,128)} %param.16) | copy-start | bytes 19204
  270.8 32.2 %copy-start.46 = (f32[1024]{0:T(1024)S(1)}, f32[1024]{0:T(1024)}, u32[]{:S(2)}) copy-start(f32[1024]{0:T(1024)} %param.26) | copy-start | bytes 12292
  270.8 32.4 %copy-start.52 = (f32[1024]{0:T(1024)S(1)}, f32[1024]{0:T(1024)}, u32[]{:S(2)}) copy-start(f32[1024]{0:T(1024)} %pad_maximum_fusion.2) | copy-start | bytes 12292
  271.1 32.7 %copy-start.42 = (f32[1024]{0:T(1024)S(1)}, f32[1024]{0:T(1024)}, u32[]{:S(2)}) copy-start(f32[1024]{0:T(1024)} %param.21) | copy-start | bytes 12292
  271.1 33.4 %copy-start.1 = (bf16[1024,1024]{1,0:T(8,128)(2,1)S(1)}, bf16[1024,1024]{1,0:T(8,128)(2,1)}, u32[]{:S(2)}) copy-start(bf16[1024,1024]{1,0:T(8,128)(2,1)} %all-gather.8.cloned.1.call-done) | copy-start | bytes 6291460
  303.2 1.8 copy-start.8
  303.2 1.8 copy-start.13
  304.4 3.2 copy-start.25
  304.9 2.7 copy-start.4
  310.2 7.4 %copy-start.3 = (bf16[1024,512]{1,0:T(8,128)(2,1)S(1)}, bf16[1024,512]{1,0:T(8,128)(2,1)}, u32[]{:S(2)}) copy-start(bf16[1024,512]{1,0:T(8,128)(2,1)} %all-gather.12.cloned.1.call-done) | copy-start | bytes 3145732
  310.2 7.4 %copy-start.26 = (bf16[50,1024]{1,0:T(8,128)(2,1)S(1)}, bf16[50,1024]{1,0:T(8,128)(2,1)}, u32[]{:S(2)}) copy-start(bf16[50,1024]{1,0:T(8,128)(2,1)} %copy-done.25) | copy-start | bytes 307204
  313.3 2.0 copy-start.37
  315.4 2.1 copy-start.57
  323.6 2.3 copy-start.31
  323.6 2.3 copy-start.47
  323.6 2.5 copy-start.51
  323.6 3.7 %copy-start.43 = (f32[1024]{0:T(1024)S(1)}, f32[1024]{0:T(1024)}, u32[]{:S(2)}) copy-start(f32[1024]{0:T(1024)} %param.21) | copy-start | bytes 12292
  326.1 1.9 copy-start.40
  326.2 1.9 copy-start.9
  326.2 1.9 copy-start.14
  327.4 2.7 copy-start.27
  327.9 2.2 copy-start.5
  332.6 6.7 %copy-start.28 = (bf16[50,1024]{1,0:T(8,128)(2,1)S(1)}, bf16[50,1024]{1,0:T(8,128)(2,1)}, u32[]{:S(2)}) copy-start(bf16[50,1024]{1,0:T(8,128)(2,1)} %copy-done.27) | copy-start | bytes 307204
  345.3 2.2 copy-start.32
  348.5 3.3 copy-start.10
  348.5 3.3 copy-start.15
  351.8 1.6 copy-start.11
  351.9 1.6 copy-start.16
  353.3 3.4 copy-start.24
  354.5 5.5 %copy-start.2 = (bf16[1024,1024]{1,0:T(8,128)(2,1)S(1)}, bf16[1024,1024]{1,0:T(8,128)(2,1)}, u32[]{:S(2)}) copy-start(bf16[1024,1024]{1,0:T(8,128)(2,1)} %all-gather.14.cloned.1.call-done) | copy-start | bytes 6291460
  354.5 5.5 %copy-start.20 = (f32[50,1024]{1,0:T(8,128)S(1)}, f32[50,1024]{1,0:T(8,128)}, u32[]{:S(2)}) copy-start(f32[50,1024]{1,0:T(8,128)} %copy-done.19) | copy-start | bytes 614404
  357.6 2.9 copy-start.33
  357.6 2.9 copy-start.48
  (16 other events, 17.1 us)
Sparse Core Ops, SparseCore 0:
  9.5 40.6 all-gather.9
  52.4 36.8 all-gather.11
  91.4 40.4 all-gather.7
  133.9 125.1 all-gather.5
  261.1 39.6 all-gather.13
where the time goes:
time: 369 us; the launch traced here: 368 us
  waiting for transfers between devices  266 us (72%)
  matrix products  50.5 us (14%)
  local copies, waits for them, and re-layouts  20.1 us (5%)
  other arithmetic  16.4 us (4%)
  between operations  15.1 us (4%)
    all_gather x1, waiting for transfers between devices, shards(): lax.all_gather(stacked, 'wide', axis=1, tiled=True)  124 us
    all_gather x1, waiting for transfers between devices, shards(): lax.all_gather(expert_query, 'wide', axis=0, tiled=True)  40.4 us
    all_gather x1, waiting for transfers between devices, shards(): lax.all_gather(expert_value, 'wide', axis=0, tiled=True)  37.4 us
    all_gather x1, waiting for transfers between devices, shards(): lax.all_gather(expert_key, 'wide', axis=0, tiled=True)  31.2 us
    all_gather x1, waiting for transfers between devices, shards(): lax.all_gather(expert_output, 'wide', axis=0, tiled=True)  29.5 us
    dot_general x1, matrix products, shards(): jnp.einsum('pd,kdc->pkc', normed, lax.all_gather(stacked, 'wide', axis=1,...  9.54 us
  transfers between devices with their start and end apart: 5, of which 5 were waited for; matrix products, arithmetic and copies ran while one was open for 7% of the time, Pallas kernels for 0%

commit v1 on v0

--- a/solution.py
+++ b/solution.py
@@ -1,3 +1,4 @@
+import functools
 import jax
 import jax.numpy as jnp
 from jax import lax
@@ -7,6 +8,31 @@
 STEPS = 4
 rope_base = 1000000.0
 norm_eps = 1e-06
+
+
+def scan_flows(u, on_dim):
+    val = list(u.shape[1:])
+    val[on_dim] *= u.shape[0]
+    return jnp.moveaxis(u, 0, on_dim).reshape(val)
+
+
+def recast_ends_up(panel, a_name, pos_dim):
+    buffer = []
+    k_all = lax.psum(1, a_name)
+    src_i = 0
+    while src_i < k_all:
+        buffer.append((src_i, (src_i + 1) % k_all))
+        src_i = src_i + 1
+    gallery = [panel]
+    while len(gallery) < k_all:
+        p_next = lax.ppermute(gallery[-1], a_name, buffer)
+        gallery.append(p_next)
+    arr_out = lax.axis_index(a_name)
+    gallery = jnp.stack(gallery, 0)[(arr_out - jnp.arange(k_all)) % k_all]
+    return scan_flows(gallery, pos_dim)
+
+
+keep_up_fields = functools.partial(recast_ends_up, a_name="wide", pos_dim=0)
 
 
 def normalize(values, norm_gain):
@@ -133,7 +159,7 @@
     gathered = (
         lax.all_gather(expert_query, "wide", axis=0, tiled=True),
         lax.all_gather(expert_key, "wide", axis=0, tiled=True),
-        lax.all_gather(expert_value, "wide", axis=0, tiled=True),
+        keep_up_fields(expert_value),
         lax.all_gather(expert_output, "wide", axis=0, tiled=True),
     )
     hidden = prefix_hidden[0]

time: 369 us -> 333 us (0.902)
  waiting for transfers between devices: 266 us -> 226 us
    ppermute x0 -> x15, waiting for transfers between devices: none -> 91.8 us  [recast_ends_up(): p_next = lax.ppermute(gallery[-1], a_name, buffer)]
    all_gather x1, waiting for transfers between devices: 40.4 us -> 0.02 us  [shards(): lax.all_gather(expert_query, 'wide', axis=0, tiled=True)]
    all_gather x1 -> x0, waiting for transfers between devices: 37.4 us -> none  [shards(): lax.all_gather(expert_value, 'wide', axis=0, tiled=True)]
    all_gather x1, waiting for transfers between devices: 31.2 us -> 0.02 us  [shards(): lax.all_gather(expert_key, 'wide', axis=0, tiled=True)]
    all_gather x1, waiting for transfers between devices: 124 us -> 104 us  [shards(): lax.all_gather(stacked, 'wide', axis=1, tiled=True)]
  transfers between devices with their start and end apart: 5 -> 19, of which waited for: 5 -> 16; matrix products, arithmetic and copies ran while one was open for 7% -> 8% of each run, Pallas kernels for 0% -> 0%
where the time goes in v1:
time: 333 us; the launch traced here: 331 us
  waiting for transfers between devices  226 us (68%)
  matrix products  49.4 us (15%)
  local copies, waits for them, and re-layouts  20.2 us (6%)
  other arithmetic  17.1 us (5%)
  between operations  15.1 us (5%)
  starting transfers between devices  3.37 us (1%)
    all_gather x1, waiting for transfers between devices, shards(): lax.all_gather(stacked, 'wide', axis=1, tiled=True)  104 us
    ppermute x15, waiting for transfers between devices, recast_ends_up(): p_next = lax.ppermute(gallery[-1], a_name, buffer)  91.8 us
    all_gather x1, waiting for transfers between devices, shards(): lax.all_gather(expert_output, 'wide', axis=0, tiled=True)  29 us
    dot_general x1, matrix products, shards(): jnp.einsum('pd,kdc->pkc', normed, lax.all_gather(stacked, 'wide', axis=1,...  9.59 us
    dot_general x4, matrix products, expert_steps(): jnp.dot(attn_mixed, output_w, preferred_element_type=jnp.float32)  7.24 us
  transfers between devices with their start and end apart: 19, of which 16 were waited for; matrix products, arithmetic and copies ran while one was open for 8% of the time, Pallas kernels for 0%

profile of v1, /device:TPU:0, one launch (start us, length us, event | category | flops | bytes accessed | tf_op | source)
XLA Modules:
  0.0 331.4 jit_solution(3031819663181391979)
XLA Ops:
  8.1 2.3 pad_maximum_fusion
  11.3 3.1 fusion
  18.4 2.7 collective-permute-start.1
  21.0 4.9 %collective-permute-done.1 = bf16[64,512]{1,0:T(8,128)(2,1)S(1)} collective-permute-done((bf16[64,512]{1,0:T(8,128)(2,1)S(1)}, bf16[64,512]{1,0:T(8,128)(2,1)S(1)}, u32[]{:S(2)}, u32[]{:S(2)}) %collective-permute-start.1) | collective-permute-done | bytes 65568 | tf_op jit(solution)/shard_map/ppermute | solution.py:28
  25.9 6.4 %collective-permute-done.2 = bf16[64,512]{1,0:T(8,128)(2,1)S(1)} collective-permute-done((bf16[64,512]{1,0:T(8,128)(2,1)S(1)}, bf16[64,512]{1,0:T(8,128)(2,1)S(1)}, u32[]{:S(2)}, u32[]{:S(2)}) %collective-permute-start.2) | collective-permute-done | bytes 65568 | tf_op jit(solution)/shard_map/ppermute | solution.py:28
  32.4 6.4 %collective-permute-done.3 = bf16[64,512]{1,0:T(8,128)(2,1)S(1)} collective-permute-done((bf16[64,512]{1,0:T(8,128)(2,1)S(1)}, bf16[64,512]{1,0:T(8,128)(2,1)S(1)}, u32[]{:S(2)}, u32[]{:S(2)}) %collective-permute-start.3) | collective-permute-done | bytes 65568 | tf_op jit(solution)/shard_map/ppermute | solution.py:28
  38.8 6.6 %collective-permute-done.4 = bf16[64,512]{1,0:T(8,128)(2,1)S(1)} collective-permute-done((bf16[64,512]{1,0:T(8,128)(2,1)S(1)}, bf16[64,512]{1,0:T(8,128)(2,1)S(1)}, u32[]{:S(2)}, u32[]{:S(2)}) %collective-permute-start.4) | collective-permute-done | bytes 65568 | tf_op jit(solution)/shard_map/ppermute | solution.py:28
  45.4 6.4 %collective-permute-done.5 = bf16[64,512]{1,0:T(8,128)(2,1)S(1)} collective-permute-done((bf16[64,512]{1,0:T(8,128)(2,1)S(1)}, bf16[64,512]{1,0:T(8,128)(2,1)S(1)}, u32[]{:S(2)}, u32[]{:S(2)}) %collective-permute-start.5) | collective-permute-done | bytes 65568 | tf_op jit(solution)/shard_map/ppermute | solution.py:28
  51.8 6.4 %collective-permute-done.6 = bf16[64,512]{1,0:T(8,128)(2,1)S(1)} collective-permute-done((bf16[64,512]{1,0:T(8,128)(2,1)S(1)}, bf16[64,512]{1,0:T(8,128)(2,1)S(1)}, u32[]{:S(2)}, u32[]{:S(2)}) %collective-permute-start.6) | collective-permute-done | bytes 65568 | tf_op jit(solution)/shard_map/ppermute | solution.py:28
  58.2 6.5 %collective-permute-done.7 = bf16[64,512]{1,0:T(8,128)(2,1)S(1)} collective-permute-done((bf16[64,512]{1,0:T(8,128)(2,1)S(1)}, bf16[64,512]{1,0:T(8,128)(2,1)S(1)}, u32[]{:S(2)}, u32[]{:S(2)}) %collective-permute-start.7) | collective-permute-done | bytes 65568 | tf_op jit(solution)/shard_map/ppermute | solution.py:28
  64.7 7.1 %collective-permute-done.8 = bf16[64,512]{1,0:T(8,128)(2,1)S(1)} collective-permute-done((bf16[64,512]{1,0:T(8,128)(2,1)S(1)}, bf16[64,512]{1,0:T(8,128)(2,1)S(1)}, u32[]{:S(2)}, u32[]{:S(2)}) %collective-permute-start.8) | collective-permute-done | bytes 65568 | tf_op jit(solution)/shard_map/ppermute | solution.py:28
  71.8 6.4 %collective-permute-done.9 = bf16[64,512]{1,0:T(8,128)(2,1)S(1)} collective-permute-done((bf16[64,512]{1,0:T(8,128)(2,1)S(1)}, bf16[64,512]{1,0:T(8,128)(2,1)S(1)}, u32[]{:S(2)}, u32[]{:S(2)}) %collective-permute-start.9) | collective-permute-done | bytes 65568 | tf_op jit(solution)/shard_map/ppermute | solution.py:28
  78.2 7.9 %collective-permute-done.10 = bf16[64,512]{1,0:T(8,128)(2,1)S(1)} collective-permute-done((bf16[64,512]{1,0:T(8,128)(2,1)S(1)}, bf16[64,512]{1,0:T(8,128)(2,1)S(1)}, u32[]{:S(2)}, u32[]{:S(2)}) %collective-permute-start.10) | collective-permute-done | bytes 65568 | tf_op jit(solution)/shard_map/ppermute | solution.py:28
  86.1 6.4 %collective-permute-done.11 = bf16[64,512]{1,0:T(8,128)(2,1)S(1)} collective-permute-done((bf16[64,512]{1,0:T(8,128)(2,1)S(1)}, bf16[64,512]{1,0:T(8,128)(2,1)S(1)}, u32[]{:S(2)}, u32[]{:S(2)}) %collective-permute-start.11) | collective-permute-done | bytes 65568 | tf_op jit(solution)/shard_map/ppermute | solution.py:28
  92.5 6.4 %collective-permute-done.12 = bf16[64,512]{1,0:T(8,128)(2,1)S(1)} collective-permute-done((bf16[64,512]{1,0:T(8,128)(2,1)S(1)}, bf16[64,512]{1,0:T(8,128)(2,1)S(1)}, u32[]{:S(2)}, u32[]{:S(2)}) %collective-permute-start.12) | collective-permute-done | bytes 65568 | tf_op jit(solution)/shard_map/ppermute | solution.py:28
  98.9 6.4 %collective-permute-done.13 = bf16[64,512]{1,0:T(8,128)(2,1)S(1)} collective-permute-done((bf16[64,512]{1,0:T(8,128)(2,1)S(1)}, bf16[64,512]{1,0:T(8,128)(2,1)S(1)}, u32[]{:S(2)}, u32[]{:S(2)}) %collective-permute-start.13) | collective-permute-done | bytes 65568 | tf_op jit(solution)/shard_map/ppermute | solution.py:28
  105.3 7.7 %collective-permute-done.14 = bf16[64,512]{1,0:T(8,128)(2,1)S(1)} collective-permute-done((bf16[64,512]{1,0:T(8,128)(2,1)S(1)}, bf16[64,512]{1,0:T(8,128)(2,1)S(1)}, u32[]{:S(2)}, u32[]{:S(2)}) %collective-permute-start.14) | collective-permute-done | bytes 65568 | tf_op jit(solution)/shard_map/ppermute | solution.py:28
  114.0 1.5 fusion.109
  115.8 2.1 fusion.108
  118.5 104.0 %all-gather.5.cloned.1.call-done = bf16[2,8192,512]{2,1,0:T(8,128)(2,1)} async-done(((bf16[2,512,512]{2,1,0:T(8,128)(2,1)}), bf16[2,8192,512]{2,1,0:T(8,128)(2,1)}) %all-gather.5.cloned.1.call-update) | async-done | bytes 16777232 | tf_op jit(solution)/shard_map/all_gather | solution.py:172
  222.5 9.6 %fusion.4 = f32[256,2,512]{2,0,1:T(8,128)S(1)} fusion(bf16[2,8192,512]{2,1,0:T(8,128)(2,1)} %all-gather.5.cloned.1.call-done, bf16[1,256,8192]{2,1,0:T(8,128)(2,1)} %param.14, f32[8192]{0:T(1024)S(1)} %copy-done.46, f32[256]{0:T(256)S(1)} %add_rsqrt_fusion), kind=kOutput, calls=%fused_computation.7 | convolution fusion | flops 4303355904 | bytes 22053888 | tf_op jit(solution)/shard_map/pd,kdc->pkc/dot_general | solution.py:169
  235.2 29.0 %all-gather.11.cloned.1.call-done = bf16[1024,1024]{1,0:T(8,128)(2,1)} async-done(((bf16[64,1024]{1,0:T(8,128)(2,1)}), bf16[1024,1024]{1,0:T(8,128)(2,1)}) %all-gather.11.cloned.1.call-update) | async-done | bytes 2097168 | tf_op jit(solution)/shard_map/all_gather | solution.py:163
  264.2 2.2 multiply_reduce_fusion.6
  266.4 1.0 fusion.25
  267.4 1.2 multiply_reduce_fusion.5
  272.5 1.7 fusion.102
  275.1 1.6 reshape.364
  276.7 1.1 fusion.98
  278.6 1.2 fusion.103
  280.5 1.3 fusion.27
  282.5 2.1 fusion.31
  284.6 1.5 reshape.365
  286.1 1.3 fusion.19
  288.1 1.6 convert_element_type.174
  289.7 2.2 multiply_reduce_fusion.4
  296.0 1.1 fusion.104
  298.0 1.6 reshape.367
  299.6 1.1 fusion.97
  301.5 1.2 fusion.105
  302.7 1.4 fusion.28
  304.2 2.1 fusion.32
  306.3 1.5 reshape.368
  307.7 1.3 fusion.18
  309.8 1.6 convert_element_type.184
  311.3 2.2 multiply_reduce_fusion.2
  314.6 1.2 multiply_reduce_fusion.1
  321.1 1.0 fusion.33
  322.1 1.2 fusion.17
  (243 shorter events, 32.2 us)
Async XLA Ops:
  6.5 8.4 %copy-start = (f32[32,1024]{1,0:T(8,128)S(1)}, f32[32,1024]{1,0:T(8,128)}, u32[]{:S(2)}) copy-start(f32[32,1024]{1,0:T(8,128)} %param.20) | copy-start | bytes 393220
  6.5 3.9 %copy-start.35 = (bf16[64,512]{1,0:T(8,128)(2,1)S(1)}, bf16[64,512]{1,0:T(8,128)(2,1)}, u32[]{:S(2)}) copy-start(bf16[64,512]{1,0:T(8,128)(2,1)} %param.24) | copy-start | bytes 196612
  6.5 107.5 %all-gather.9.cloned.1.call-start = ((), (), s32[]{:S(2)}) async-start(), calls=%async_computation.2 | async-start | bytes 1114112 | tf_op jit(solution)/shard_map/all_gather | solution.py:161
  7.3 108.5 %all-gather.7.cloned.1.call-start = ((), (), s32[]{:S(2)}) async-start(), calls=%async_computation.1 | async-start | bytes 2228224 | tf_op jit(solution)/shard_map/all_gather | solution.py:160
  8.0 214.5 %all-gather.5.cloned.1.call-start = ((), (), s32[]{:S(2)}) async-start(), calls=%async_computation | async-start | bytes 17825792 | tf_op jit(solution)/shard_map/all_gather | solution.py:172
  10.4 253.8 %all-gather.11.cloned.1.call-start = ((), (), s32[]{:S(2)}) async-start(), calls=%async_computation.3 | async-start | bytes 2228224 | tf_op jit(solution)/shard_map/all_gather | solution.py:163
  10.4 7.9 %collective-permute-start = (bf16[64,512]{1,0:T(8,128)(2,1)S(1)}, bf16[64,512]{1,0:T(8,128)(2,1)S(1)}, u32[]{:S(2)}, u32[]{:S(2)}) collective-permute-start(bf16[64,512]{1,0:T(8,128)(2,1)S(1)} %copy-done.35), channel_id=1, source_target_pairs={{0,1},{1,2},{2,3},{3,4},{4,5},{5,6},{6,7},{7,8},{8,9},{9,10},{10,1... | collective-permute-start | bytes 196616 | tf_op jit(solution)/shard_map/ppermute | solution.py:28
  11.3 3.7 %copy-start.36 = (f32[1,50,32]{1,2,0:T(8,128)S(1)}, f32[1,50,32]{1,2,0:T(8,128)}, u32[]{:S(2)}) copy-start(f32[1,50,32]{1,2,0:T(8,128)} %param.16) | copy-start | bytes 19204
  11.3 6.9 %copy-start.33 = (f32[1024]{0:T(1024)S(1)}, f32[1024]{0:T(1024)}, u32[]{:S(2)}) copy-start(f32[1024]{0:T(1024)} %param.21) | copy-start | bytes 12292
  15.5 97.6 %copy-start.16 = (f32[50,1024]{1,0:T(8,128)}, f32[50,1024]{1,0:T(8,128)S(1)}, u32[]{:S(2)}) copy-start(f32[50,1024]{1,0:T(8,128)S(1)} %get-tuple-element.38) | copy-start | bytes 614404
  16.4 101.6 %copy-start.6 = (f32[50,64]{1,0:T(8,128)}, f32[50,64]{1,0:T(8,128)S(1)}, u32[]{:S(2)}) copy-start(f32[50,64]{1,0:T(8,128)S(1)} %get-tuple-element.33) | copy-start | bytes 38404
  16.4 101.6 %copy-start.11 = (f32[50,64]{1,0:T(8,128)}, f32[50,64]{1,0:T(8,128)S(1)}, u32[]{:S(2)}) copy-start(f32[50,64]{1,0:T(8,128)S(1)} %get-tuple-element.34) | copy-start | bytes 38404
  18.3 214.8 %copy-start.41 = (pred[256]{0:T(512)(128)(4,1)}, pred[256]{0:T(512)(128)(4,1)S(1)}, u32[]{:S(2)}) copy-start(pred[256]{0:T(512)(128)(4,1)S(1)} %iota_compare_fusion) | copy-start | bytes 772
  18.4 7.6 %collective-permute-start.1 = (bf16[64,512]{1,0:T(8,128)(2,1)S(1)}, bf16[64,512]{1,0:T(8,128)(2,1)S(1)}, u32[]{:S(2)}, u32[]{:S(2)}) collective-permute-start(bf16[64,512]{1,0:T(8,128)(2,1)S(1)} %collective-permute-done), channel_id=1, source_target_pairs={{0,1},{1,2},{2,3},{3,4},{4,5},{5,6},{6,7},{7,8},{8,9},{9,10},{10,1... | collective-permute-start | bytes 196616 | tf_op jit(solution)/shard_map/ppermute | solution.py:28
  25.9 6.4 %collective-permute-start.2 = (bf16[64,512]{1,0:T(8,128)(2,1)S(1)}, bf16[64,512]{1,0:T(8,128)(2,1)S(1)}, u32[]{:S(2)}, u32[]{:S(2)}) collective-permute-start(bf16[64,512]{1,0:T(8,128)(2,1)S(1)} %collective-permute-done.1), channel_id=1, source_target_pairs={{0,1},{1,2},{2,3},{3,4},{4,5},{5,6},{6,7},{7,8},{8,9},{9,10},{10,1... | collective-permute-start | bytes 196616 | tf_op jit(solution)/shard_map/ppermute | solution.py:28
  32.4 6.4 %collective-permute-start.3 = (bf16[64,512]{1,0:T(8,128)(2,1)S(1)}, bf16[64,512]{1,0:T(8,128)(2,1)S(1)}, u32[]{:S(2)}, u32[]{:S(2)}) collective-permute-start(bf16[64,512]{1,0:T(8,128)(2,1)S(1)} %collective-permute-done.2), channel_id=1, source_target_pairs={{0,1},{1,2},{2,3},{3,4},{4,5},{5,6},{6,7},{7,8},{8,9},{9,10},{10,1... | collective-permute-start | bytes 196616 | tf_op jit(solution)/shard_map/ppermute | solution.py:28
  38.8 6.6 %collective-permute-start.4 = (bf16[64,512]{1,0:T(8,128)(2,1)S(1)}, bf16[64,512]{1,0:T(8,128)(2,1)S(1)}, u32[]{:S(2)}, u32[]{:S(2)}) collective-permute-start(bf16[64,512]{1,0:T(8,128)(2,1)S(1)} %collective-permute-done.3), channel_id=1, source_target_pairs={{0,1},{1,2},{2,3},{3,4},{4,5},{5,6},{6,7},{7,8},{8,9},{9,10},{10,1... | collective-permute-start | bytes 196616 | tf_op jit(solution)/shard_map/ppermute | solution.py:28
  45.4 6.4 %collective-permute-start.5 = (bf16[64,512]{1,0:T(8,128)(2,1)S(1)}, bf16[64,512]{1,0:T(8,128)(2,1)S(1)}, u32[]{:S(2)}, u32[]{:S(2)}) collective-permute-start(bf16[64,512]{1,0:T(8,128)(2,1)S(1)} %collective-permute-done.4), channel_id=1, source_target_pairs={{0,1},{1,2},{2,3},{3,4},{4,5},{5,6},{6,7},{7,8},{8,9},{9,10},{10,1... | collective-permute-start | bytes 196616 | tf_op jit(solution)/shard_map/ppermute | solution.py:28
  51.8 6.4 %collective-permute-start.6 = (bf16[64,512]{1,0:T(8,128)(2,1)S(1)}, bf16[64,512]{1,0:T(8,128)(2,1)S(1)}, u32[]{:S(2)}, u32[]{:S(2)}) collective-permute-start(bf16[64,512]{1,0:T(8,128)(2,1)S(1)} %collective-permute-done.5), channel_id=1, source_target_pairs={{0,1},{1,2},{2,3},{3,4},{4,5},{5,6},{6,7},{7,8},{8,9},{9,10},{10,1... | collective-permute-start | bytes 196616 | tf_op jit(solution)/shard_map/ppermute | solution.py:28
  58.2 6.5 %collective-permute-start.7 = (bf16[64,512]{1,0:T(8,128)(2,1)S(1)}, bf16[64,512]{1,0:T(8,128)(2,1)S(1)}, u32[]{:S(2)}, u32[]{:S(2)}) collective-permute-start(bf16[64,512]{1,0:T(8,128)(2,1)S(1)} %collective-permute-done.6), channel_id=1, source_target_pairs={{0,1},{1,2},{2,3},{3,4},{4,5},{5,6},{6,7},{7,8},{8,9},{9,10},{10,1... | collective-permute-start | bytes 196616 | tf_op jit(solution)/shard_map/ppermute | solution.py:28
  64.7 7.1 %collective-permute-start.8 = (bf16[64,512]{1,0:T(8,128)(2,1)S(1)}, bf16[64,512]{1,0:T(8,128)(2,1)S(1)}, u32[]{:S(2)}, u32[]{:S(2)}) collective-permute-start(bf16[64,512]{1,0:T(8,128)(2,1)S(1)} %collective-permute-done.7), channel_id=1, source_target_pairs={{0,1},{1,2},{2,3},{3,4},{4,5},{5,6},{6,7},{7,8},{8,9},{9,10},{10,1... | collective-permute-start | bytes 196616 | tf_op jit(solution)/shard_map/ppermute | solution.py:28
  71.8 6.4 %collective-permute-start.9 = (bf16[64,512]{1,0:T(8,128)(2,1)S(1)}, bf16[64,512]{1,0:T(8,128)(2,1)S(1)}, u32[]{:S(2)}, u32[]{:S(2)}) collective-permute-start(bf16[64,512]{1,0:T(8,128)(2,1)S(1)} %collective-permute-done.8), channel_id=1, source_target_pairs={{0,1},{1,2},{2,3},{3,4},{4,5},{5,6},{6,7},{7,8},{8,9},{9,10},{10,1... | collective-permute-start | bytes 196616 | tf_op jit(solution)/shard_map/ppermute | solution.py:28
  78.2 7.9 %collective-permute-start.10 = (bf16[64,512]{1,0:T(8,128)(2,1)S(1)}, bf16[64,512]{1,0:T(8,128)(2,1)S(1)}, u32[]{:S(2)}, u32[]{:S(2)}) collective-permute-start(bf16[64,512]{1,0:T(8,128)(2,1)S(1)} %collective-permute-done.9), channel_id=1, source_target_pairs={{0,1},{1,2},{2,3},{3,4},{4,5},{5,6},{6,7},{7,8},{8,9},{9,10},{10,1... | collective-permute-start | bytes 196616 | tf_op jit(solution)/shard_map/ppermute | solution.py:28
  86.1 6.4 %collective-permute-start.11 = (bf16[64,512]{1,0:T(8,128)(2,1)S(1)}, bf16[64,512]{1,0:T(8,128)(2,1)S(1)}, u32[]{:S(2)}, u32[]{:S(2)}) collective-permute-start(bf16[64,512]{1,0:T(8,128)(2,1)S(1)} %collective-permute-done.10), channel_id=1, source_target_pairs={{0,1},{1,2},{2,3},{3,4},{4,5},{5,6},{6,7},{7,8},{8,9},{9,10},{10,1... | collective-permute-start | bytes 196616 | tf_op jit(solution)/shard_map/ppermute | solution.py:28
  92.5 6.4 %collective-permute-start.12 = (bf16[64,512]{1,0:T(8,128)(2,1)S(1)}, bf16[64,512]{1,0:T(8,128)(2,1)S(1)}, u32[]{:S(2)}, u32[]{:S(2)}) collective-permute-start(bf16[64,512]{1,0:T(8,128)(2,1)S(1)} %collective-permute-done.11), channel_id=1, source_target_pairs={{0,1},{1,2},{2,3},{3,4},{4,5},{5,6},{6,7},{7,8},{8,9},{9,10},{10,1... | collective-permute-start | bytes 196616 | tf_op jit(solution)/shard_map/ppermute | solution.py:28
  98.9 6.4 %collective-permute-start.13 = (bf16[64,512]{1,0:T(8,128)(2,1)S(1)}, bf16[64,512]{1,0:T(8,128)(2,1)S(1)}, u32[]{:S(2)}, u32[]{:S(2)}) collective-permute-start(bf16[64,512]{1,0:T(8,128)(2,1)S(1)} %collective-permute-done.12), channel_id=1, source_target_pairs={{0,1},{1,2},{2,3},{3,4},{4,5},{5,6},{6,7},{7,8},{8,9},{9,10},{10,1... | collective-permute-start | bytes 196616 | tf_op jit(solution)/shard_map/ppermute | solution.py:28
  105.3 7.7 %collective-permute-start.14 = (bf16[64,512]{1,0:T(8,128)(2,1)S(1)}, bf16[64,512]{1,0:T(8,128)(2,1)S(1)}, u32[]{:S(2)}, u32[]{:S(2)}) collective-permute-start(bf16[64,512]{1,0:T(8,128)(2,1)S(1)} %collective-permute-done.13), channel_id=1, source_target_pairs={{0,1},{1,2},{2,3},{3,4},{4,5},{5,6},{6,7},{7,8},{8,9},{9,10},{10,1... | collective-permute-start | bytes 196616 | tf_op jit(solution)/shard_map/ppermute | solution.py:28
  115.7 106.8 %copy-start.46 = (f32[8192]{0:T(1024)S(1)}, f32[8192]{0:T(1024)}, u32[]{:S(2)}) copy-start(f32[8192]{0:T(1024)} %param.17) | copy-start | bytes 98308
  235.2 35.8 %copy-start.1 = (bf16[1024,1024]{1,0:T(8,128)(2,1)S(1)}, bf16[1024,1024]{1,0:T(8,128)(2,1)}, u32[]{:S(2)}) copy-start(bf16[1024,1024]{1,0:T(8,128)(2,1)} %all-gather.7.cloned.1.call-done) | copy-start | bytes 6291460
  264.2 2.2 copy-start.21
  271.0 1.5 copy-start.42
  271.5 2.7 copy-start.3
  279.8 2.0 copy-start.27
  289.7 2.3 copy-start.22
  289.7 2.3 copy-start.37
  289.7 2.5 copy-start.40
  289.7 3.7 %copy-start.34 = (f32[1024]{0:T(1024)S(1)}, f32[1024]{0:T(1024)}, u32[]{:S(2)}) copy-start(f32[1024]{0:T(1024)} %param.21) | copy-start | bytes 12292
  294.5 1.5 copy-start.43
  295.0 2.1 copy-start.4
  311.3 2.2 copy-start.23
  318.8 1.6 copy-start.10
  318.8 1.6 copy-start.15
  319.1 2.0 copy-start.30
  320.2 1.9 copy-start.31
  321.0 2.5 copy-start.2
  321.0 2.5 copy-start.18
  322.1 2.0 copy-start.24
  322.1 2.0 copy-start.38
  (18 other events, 19.9 us)
Sparse Core Ops, SparseCore 0:
  9.5 40.9 all-gather.8
  52.6 41.8 all-gather.6
  96.7 125.7 all-gather.4
  224.5 39.6 all-gather.10
